TPU v7x, 256 devices: a whole 4x4x8 slice. The times are simulated.
256 devices in a mesh: seq: 32 (over x, z), head: 8 (over y, core).
Axes of the slice: x: 4, y: 4, z: 8, core: 2. Of those that a mesh axis runs over, the one named last changes fastest.
Arguments:
- query_projection: bfloat16 [8192, 4096], P(('seq', 'head')), may hold values from -6 to 6
- key_projection: bfloat16 [8192, 1024], P(('seq', 'head')), may hold values from -6 to 6
- value_projection: bfloat16 [8192, 1024], P(('seq', 'head')), may hold values from -6 to 6
- output_gradient: bfloat16 [8192, 4096], P(('seq', 'head')), may hold values from -6 to 6
- partners: int32 [64, 6], P('seq'), may hold values from -1 to 62, as said below
Outputs:
- attention: bfloat16 [8192, 4096], P('seq', 'head')
- grad_query: bfloat16 [8192, 4096], P('seq', 'head')
- key_gradient: bfloat16 [8192, 1024], P('seq', 'head')
- value_gradient: bfloat16 [8192, 1024], P('seq', 'head')
Inputs may be any that keep to these rules, and one draw needn't show every extreme that they name: For l < 1, partners[b, l] is -1 if b < 2**l, else a block at a distance of 2**l to 2**(l+1) - 1 blocks before b (not before block 0). For l = 1 + j, with g = b // 2 - 2**j, it is -1 if g < 0, else one of the blocks g * 2 to g * 2 + 1.
All inputs are finite; a program needn't handle non-finite values.
Results may differ from a plain program's by a relative error of at most 0.012.
Values may be sent and summed in bfloat16 or wider, within the bound.
No kernel may reach another device: no remote copies, remote signals or barrier semaphores. Data moves between devices by JAX's collectives and lax.ppermute only.
A program may use at most 64 MiB of HBM per device.

v0:
```python
import math
import jax
import jax.numpy as jnp
from jax import lax
from jax.sharding import PartitionSpec as P

HEAD_SIZE = 128
BLOCK_TOKENS = 128
masked_score = -1e30


def from_behind(value, axis, steps):
    count = lax.axis_size(axis)
    initial, last = (max(0, -steps), min(count, count - steps))
    return lax.ppermute(value, axis, [(source, source + steps) for source in range(initial, last)])


def shards(query_projection, key_projection, value_projection, output_gradient, partners):
    q_local, dout_local, k_local, v_local = (
        lax.all_to_all(query_projection, "head", split_axis=1, concat_axis=0, tiled=True),
        lax.all_to_all(output_gradient, "head", split_axis=1, concat_axis=0, tiled=True),
        lax.all_to_all(key_projection, "head", split_axis=1, concat_axis=0, tiled=True),
        lax.all_to_all(value_projection, "head", split_axis=1, concat_axis=0, tiled=True),
    )
    tokens_dev = q_local.shape[0]
    block_count = tokens_dev // BLOCK_TOKENS
    q_heads = q_local.shape[1] // HEAD_SIZE
    kv_heads = k_local.shape[1] // HEAD_SIZE
    heads_per_group = q_heads // kv_heads
    level_list = partners.shape[1]
    near_count = block_count.bit_length() - 1
    far_count = level_list - near_count
    scaling = 1.0 / math.sqrt(HEAD_SIZE)
    highest = lax.Precision.HIGHEST
    key_value = jnp.stack([k_local, v_local])
    far_sets = [from_behind(key_value, "seq", 2**degree) for degree in range(far_count)]
    block_shape = (2, block_count, BLOCK_TOKENS, kv_heads * HEAD_SIZE)
    own_blocks = key_value.reshape(block_shape)
    near_pool = jnp.concatenate([far_sets[0].reshape(block_shape), own_blocks], axis=1)
    first_block = lax.axis_index("seq") * block_count
    is_valid = partners >= 0
    picked = [own_blocks]
    degree = 0
    target = partners[:, degree] - first_block + block_count
    near_targets = target
    picked.append(jnp.take(near_pool, jnp.clip(target, 0, 2 * block_count - 1), axis=1))
    far_targets = []
    for degree in range(far_count):
        target = partners[:, near_count + degree] - (first_block - 2**degree * block_count)
        far_targets.append(target)
        picked.append(
            jnp.take(
                far_sets[degree].reshape(block_shape), jnp.clip(target, 0, block_count - 1), axis=1
            )
        )
    slot_count_all = 1 + level_list
    key_number = slot_count_all * BLOCK_TOKENS
    gathered = jnp.stack(picked, axis=2).reshape(2, block_count, key_number, kv_heads, HEAD_SIZE)
    row_ids = jnp.arange(BLOCK_TOKENS)[:, None]
    columns = jnp.arange(key_number)[None, :]
    slot_of = columns // BLOCK_TOKENS
    causal = (slot_of == 0) & (columns <= row_ids)
    slot_valid = jnp.concatenate([jnp.ones((block_count, 1), bool), is_valid], axis=1)
    allowed = causal[None] | (slot_of > 0)[None] & slot_valid[:, slot_of[0]][:, None, :]
    query_blocks = q_local.reshape(block_count, BLOCK_TOKENS, q_heads, HEAD_SIZE)
    output_grad_blocks = dout_local.reshape(block_count, BLOCK_TOKENS, q_heads, HEAD_SIZE)
    attn_list = []
    dquery_list = []
    key_row_set = gathered[0, :, :, 0, :]
    value_row_set = gathered[1, :, :, 0, :]
    key_sum = jnp.zeros((block_count, key_number, HEAD_SIZE), jnp.float32)
    value_sum = jnp.zeros((block_count, key_number, HEAD_SIZE), jnp.float32)
    for member in range(heads_per_group):
        query_row_set = query_blocks[:, :, member, :]
        output_grad_rows = output_grad_blocks[:, :, member, :]
        scores = scaling * jnp.einsum(
            "frc,fzc->frz", query_row_set, key_row_set, preferred_element_type=jnp.float32
        )
        scores = jnp.where(allowed, scores, masked_score)
        row_max = jnp.max(scores, axis=-1, keepdims=True)
        exp_scores = jnp.exp(scores - row_max)
        weights = exp_scores / jnp.sum(exp_scores, axis=-1, keepdims=True)
        weights_reduced = weights.astype(jnp.bfloat16)
        attn = jnp.einsum(
            "awv,avq->awq", weights_reduced, value_row_set, preferred_element_type=jnp.float32
        )
        row_dot = jnp.sum(output_grad_rows.astype(jnp.float32) * attn, axis=-1, keepdims=True)
        dweights = jnp.einsum(
            "frc,fzc->frz", output_grad_rows, value_row_set, preferred_element_type=jnp.float32
        )
        score_gradient = (weights * (dweights - row_dot)).astype(jnp.bfloat16)
        dquery = scaling * jnp.einsum(
            "awv,avq->awq", score_gradient, key_row_set, preferred_element_type=jnp.float32
        )
        key_sum = key_sum + scaling * jnp.einsum(
            "ioc,ioa->ica", score_gradient, query_row_set, preferred_element_type=jnp.float32
        )
        value_sum = value_sum + jnp.einsum(
            "ioc,ioa->ica", weights_reduced, output_grad_rows, preferred_element_type=jnp.float32
        )
        attn_list.append(attn)
        dquery_list.append(dquery)
    key_grads = [key_sum]
    value_grads = [value_sum]
    grads = jnp.stack([jnp.stack(key_grads, axis=2), jnp.stack(value_grads, axis=2)])
    grads = grads.reshape(2, block_count, slot_count_all, BLOCK_TOKENS * kv_heads * HEAD_SIZE)
    positions = jnp.arange(2 * block_count)[None, :]
    near_hot = jnp.stack(
        [((near_targets[:, None] == positions) & is_valid[:, 0:1]).astype(jnp.float32)]
    )
    near_sum = jnp.einsum(
        "lqp,sqlx->spx", near_hot, grads[:, :, 1 : 1 + near_count], precision=highest
    )
    own_total = grads[:, :, 0] + near_sum[:, block_count:]
    local_ids = jnp.arange(block_count)[None, :]
    far_parts = []
    for degree in range(far_count):
        column = near_count + degree
        one_hot = (
            (far_targets[degree][:, None] == local_ids) & is_valid[:, column : column + 1]
        ).astype(jnp.float32)
        far_part = jnp.einsum("qp,sqx->spx", one_hot, grads[:, :, 1 + column], precision=highest)
        if degree == 0:
            far_part = far_part + near_sum[:, :block_count]
        far_parts.append(far_part)
    summed = own_total
    for degree in range(far_count):
        summed = summed + from_behind(far_parts[degree], "seq", -(2**degree))
    kv_out = summed.reshape(2, tokens_dev, kv_heads * HEAD_SIZE).astype(jnp.bfloat16)
    attention = (
        jnp.stack(attn_list, axis=2).reshape(tokens_dev, q_heads * HEAD_SIZE).astype(jnp.bfloat16)
    )
    grad_query = (
        jnp.stack(dquery_list, axis=2).reshape(tokens_dev, q_heads * HEAD_SIZE).astype(jnp.bfloat16)
    )
    return (attention, grad_query, kv_out[0], kv_out[1])


def solution(mesh):
    placed = (
        P(("seq", "head"), None),
        P(("seq", "head"), None),
        P(("seq", "head"), None),
        P(("seq", "head"), None),
        P("seq", None),
    )
    return jax.shard_map(
        shards,
        mesh=mesh,
        in_specs=placed,
        out_specs=(P("seq", "head"), P("seq", "head"), P("seq", "head"), P("seq", "head")),
        check_vma=False,
    )
```

profile of v0, /device:TPU:2, one launch (start us, length us, event | category | flops | bytes accessed | tf_op | source)
XLA Modules:
  0.0 144.5 jit_solution(5050257627439415097)
XLA Ops:
  2.1 4.5 %all-to-all-start = ((bf16[32,8,128]{2,0,1:T(8,128)(2,1)}), bf16[32,8,128]{2,0,1:T(8,128)(2,1)S(1)}, u32[]{:S(2)}, u32[]{:S(2)}) async-start(bf16[32,8,128]{2,0,1:T(8,128)(2,1)} %copy_bitcast_fusion.5), calls=%async_computation | async-start | bytes 131072 | tf_op jit(solution)/shard_map/all_to_all | solution.py:22
  7.4 1.7 %fusion.95 = (s32[2]{0:T(128)S(1)}, s32[2]{0:T(128)S(1)}, s32[2]{0:T(128)}, s32[2]{0:T(128)}, s32[2]{0:T(128)}, /*index=5*/s32[2]{0:T(128)}, s32[2]{0:T(128)S(1)...) fusion(s32[2,6]{1,0:T(2,128)} %param.11, s32[]{:T(128)S(6)} %sub.154, ...), kind=kLoop, calls=%fused_computation.221 | loop fusion | flops 32 | bytes 168 | tf_op jit(solution)/shard_map/sub | solution.py:49
  10.7 1.5 %copy_bitcast_fusion.4 = bf16[32,8,128]{2,0,1:T(8,128)(2,1)} fusion(bf16[32,1024]{1,0:T(8,128)(2,1)} %param.9), kind=kLoop, calls=%fused_computation.120 | loop fusion | bytes 131072 | tf_op jit(solution)/shard_map/all_to_all | solution.py:23
  12.9 1.7 %copy.231 = bf16[4,8,8,512]{3,2,0,1:T(8,128)(2,1)} copy(bf16[4,8,8,512]{3,2,1,0:T(8,128)(2,1)} %bitcast.345) | data formatting | bytes 524288 | tf_op jit(solution)/shard_map/all_to_all | solution.py:20
  14.6 2.2 %gather_fusion = pred[896,2]{1,0:T(8,128)(4,1)S(1)} fusion(pred[2,7]{0,1:T(8,128)(4,1)S(1)} %concatenate.9, s32[1024]{0:T(1024)S(1)} %pad_clamp_fusion.6), kind=kCustom, calls=%fused_computation.5 | custom fusion | bytes 7168 | tf_op jit(solution)/shard_map/gather | solution.py:64
  17.0 4.8 %all-to-all-start.1 = ((bf16[32,8,128]{2,0,1:T(8,128)(2,1)}), bf16[32,8,128]{2,0,1:T(8,128)(2,1)S(1)}, u32[]{:S(2)}, u32[]{:S(2)}) async-start(bf16[32,8,128]{2,0,1:T(8,128)(2,1)} %copy_bitcast_fusion.4), calls=%async_computation.1 | async-start | bytes 131072 | tf_op jit(solution)/shard_map/all_to_all | solution.py:23
  21.8 5.6 %all-to-all-done.1 = bf16[32,8,128]{2,0,1:T(8,128)(2,1)S(1)} async-done(((bf16[32,8,128]{2,0,1:T(8,128)(2,1)}), bf16[32,8,128]{2,0,1:T(8,128)(2,1)S(1)}, u32[]{:S(2)}, u32[]{:S(2)}) %all-to-all-start.1) | async-done | bytes 65568 | tf_op jit(solution)/shard_map/all_to_all | solution.py:23
  27.4 3.4 %all-to-all-start.2 = ((bf16[32,8,512]{2,0,1:T(8,128)(2,1)}), bf16[32,8,512]{2,0,1:T(8,128)(2,1)S(1)}, u32[]{:S(2)}, u32[]{:S(2)}) async-start(bf16[32,8,512]{2,0,1:T(8,128)(2,1)} %bitcast.316), calls=%async_computation.2 | async-start | bytes 524288 | tf_op jit(solution)/shard_map/all_to_all | solution.py:20
  30.8 4.0 %collective-permute-start.4 = (bf16[2,256,128]{2,1,0:T(8,128)(2,1)S(1)}, bf16[2,256,128]{2,1,0:T(8,128)(2,1)S(1)}, u32[]{:S(2)}, u32[]{:S(2)}) collective-permute-start(bf16[2,256,128]{2,1,0:T(8,128)(2,1)S(1)} %pad_maximum_fusion.2), channel_id=1, source_target_pairs={{0,128},{8,136},{16,144},{24,152},{32,160},{40,168},{48,176},{56,1... | collective-permute-start | bytes 393224 | tf_op jit(solution)/shard_map/ppermute | solution.py:15
  34.9 1.9 %collective-permute-start.3 = (bf16[2,256,128]{2,1,0:T(8,128)(2,1)S(1)}, bf16[2,256,128]{2,1,0:T(8,128)(2,1)S(1)}, u32[]{:S(2)}, u32[]{:S(2)}) collective-permute-start(bf16[2,256,128]{2,1,0:T(8,128)(2,1)S(1)} %pad_maximum_fusion.2), channel_id=1, source_target_pairs={{0,64},{8,72},{16,80},{24,88},{32,96},{40,104},{48,112},{56,120},{... | collective-permute-start | bytes 393224 | tf_op jit(solution)/shard_map/ppermute | solution.py:15
  36.8 9.1 %collective-permute-start.2 = (bf16[2,256,128]{2,1,0:T(8,128)(2,1)S(1)}, bf16[2,256,128]{2,1,0:T(8,128)(2,1)S(1)}, u32[]{:S(2)}, u32[]{:S(2)}) collective-permute-start(bf16[2,256,128]{2,1,0:T(8,128)(2,1)S(1)} %pad_maximum_fusion.2), channel_id=1, source_target_pairs={{0,32},{8,40},{16,48},{24,56},{32,64},{40,72},{48,80},{56,88},{64,... | collective-permute-start | bytes 393224 | tf_op jit(solution)/shard_map/ppermute | solution.py:15
  45.9 3.4 %collective-permute-start.1 = (bf16[2,256,128]{2,1,0:T(8,128)(2,1)S(1)}, bf16[2,256,128]{2,1,0:T(8,128)(2,1)S(1)}, u32[]{:S(2)}, u32[]{:S(2)}) collective-permute-start(bf16[2,256,128]{2,1,0:T(8,128)(2,1)S(1)} %pad_maximum_fusion.2), channel_id=1, source_target_pairs={{0,16},{8,24},{16,32},{24,40},{32,48},{40,56},{48,64},{56,72},{64,... | collective-permute-start | bytes 393224 | tf_op jit(solution)/shard_map/ppermute | solution.py:15
  49.3 2.9 %collective-permute-start = (bf16[2,256,128]{2,1,0:T(8,128)(2,1)S(1)}, bf16[2,256,128]{2,1,0:T(8,128)(2,1)S(1)}, u32[]{:S(2)}, u32[]{:S(2)}) collective-permute-start(bf16[2,256,128]{2,1,0:T(8,128)(2,1)S(1)} %pad_maximum_fusion.2), channel_id=1, source_target_pairs={{0,8},{8,16},{16,24},{24,32},{32,40},{40,48},{48,56},{56,64},{64,7... | collective-permute-start | bytes 393224 | tf_op jit(solution)/shard_map/ppermute | solution.py:15
  55.0 4.6 %collective-permute-done.1 = bf16[2,256,128]{2,1,0:T(8,128)(2,1)S(1)} collective-permute-done((bf16[2,256,128]{2,1,0:T(8,128)(2,1)S(1)}, bf16[2,256,128]{2,1,0:T(8,128)(2,1)S(1)}, u32[]{:S(2)}, u32[]{:S(2)}) %collective-permute-start.1) | collective-permute-done | bytes 131104 | tf_op jit(solution)/shard_map/ppermute | solution.py:15
  63.2 4.4 %all-to-all-start.3 = ((bf16[32,8,512]{2,0,1:T(8,128)(2,1)}), bf16[32,8,512]{2,0,1:T(8,128)(2,1)S(1)}, u32[]{:S(2)}, u32[]{:S(2)}) async-start(bf16[32,8,512]{2,0,1:T(8,128)(2,1)} %bitcast.315), calls=%async_computation.3 | async-start | bytes 524288 | tf_op jit(solution)/shard_map/all_to_all | solution.py:21
  67.9 7.3 %all-to-all-done.3 = bf16[32,8,512]{2,0,1:T(8,128)(2,1)S(1)} async-done(((bf16[32,8,512]{2,0,1:T(8,128)(2,1)}), bf16[32,8,512]{2,0,1:T(8,128)(2,1)S(1)}, u32[]{:S(2)}, u32[]{:S(2)}) %all-to-all-start.3) | async-done | bytes 262176 | tf_op jit(solution)/shard_map/all_to_all | solution.py:21
  77.2 1.6 %fusion.125 = (f32[2,128]{1,0:T(2,128)S(1)}, f32[2,128,896]{1,2,0:T(8,128)S(1)}) fusion(bf16[2,896,128]{2,1,0:T(8,128)(2,1)S(1)} %bitcast.325, pred[2,896]{1,0:T(4,128)(4,1)S(1)} %copy.119, pred[128,896]{0,1:T(8,128)(4,1)} %fusion.38, bf16[2,128,1,128]{3,2,1,0:T(2,128)(2,1)S(1)} %get-tuple-element.26), kind=kOutput, calls=%fused_computation.251 | convolution fusion | flops 59868032 | bytes 1559296 | tf_op jit(solution)/shard_map/sub | solution.py:81
  78.8 1.6 %fusion.128 = (f32[2,128]{1,0:T(2,128)S(1)}, f32[2,128,896]{1,2,0:T(8,128)S(1)}) fusion(bf16[2,896,128]{2,1,0:T(8,128)(2,1)S(1)} %bitcast.326, pred[2,896]{1,0:T(4,128)(4,1)S(1)} %copy.119, pred[128,896]{0,1:T(8,128)(4,1)} %fusion.38, bf16[2,128,1,128]{3,2,1,0:T(2,128)(2,1)S(1)} %get-tuple-element.23), kind=kOutput, calls=%fused_computation.254 | convolution fusion | flops 59868032 | bytes 1559296 | tf_op jit(solution)/shard_map/sub | solution.py:81
  81.7 1.6 %multiply_reduce_fusion.3 = (f32[2,128]{1,0:T(2,128)}, bf16[2,128,1,128]{1,3,0,2:T(8,128)(2,1)}) fusion(bf16[2,128,1,128]{1,3,0,2:T(8,128)(2,1)S(1)} %copy.182, bf16[2,128,896]{1,2,0:T(8,128)(2,1)S(1)} %fusion.39, bf16[2,896,128]{2,1,0:T(8,128)(2,1)S(1)} %bitcast.317), kind=kOutput, calls=%fused_computation.119 | convolution fusion | flops 58851072 | bytes 1049600 | tf_op jit(solution)/shard_map/awv,avq->awq/dot_general | solution.py:84
  84.4 1.5 %fusion.29 = bf16[2,128,896]{1,2,0:T(8,128)(2,1)S(1)} fusion(bf16[2,896,128]{2,1,0:T(8,128)(2,1)S(1)} %bitcast.319, f32[2,128]{1,0:T(2,128)S(1)} %get-tuple-element.35, f32[2,128,896]{1,2,0:T(8,128)} %copy-done.6, f32[2,128]{1,0:T(2,128)S(1)} %get-tuple-element.43, bf16[2,128,1,128]{1,3,0,2:T(8,128)(2,1)S(1)} %copy.185), kind=kOutput, calls=%fused_computation.60 | convolution fusion | flops 59637760 | bytes 1902592 | tf_op jit(solution)/shard_map/frc,fzc->frz/dot_general | solution.py:88
  86.8 1.4 fusion.126
  91.8 2.0 %fusion.127 = (f32[2,128]{1,0:T(2,128)}, f32[2,128,896]{1,2,0:T(8,128)}) fusion(bf16[2,896,128]{2,1,0:T(8,128)(2,1)S(1)} %bitcast.330, pred[2,896]{1,0:T(4,128)(4,1)S(1)} %copy.119, pred[128,896]{0,1:T(8,128)(4,1)S(1)} %copy-done.27, bf16[2,128,1,128]{3,2,1,0:T(2,128)(2,1)S(1)} %copy-done.15), kind=kOutput, calls=%fused_computation.253 | convolution fusion | flops 59868032 | bytes 1559296 | tf_op jit(solution)/shard_map/sub | solution.py:81
  100.9 1.4 stack.113
  102.3 1.5 %convolution_add_fusion.2 = f32[2,896,128]{2,1,0:T(8,128)S(1)} fusion(f32[2,896,128]{2,1,0:T(8,128)} %fusion.56, bf16[2,128,896]{1,2,0:T(8,128)(2,1)S(1)} %fusion.40, bf16[2,128,1,128]{1,3,0,2:T(8,128)(2,1)S(1)} %copy-done.10), kind=kOutput, calls=%fused_computation.32 | convolution fusion | flops 58949632 | bytes 2359296 | tf_op jit(solution)/shard_map/ioc,ioa->ica/dot_general | solution.py:98
  105.3 1.4 stack.114
  109.0 3.7 %collective-permute-start.6 = (f32[2,2,16384]{2,1,0:T(2,128)S(1)}, f32[2,2,16384]{2,1,0:T(2,128)S(1)}, u32[]{:S(2)}, u32[]{:S(2)}) collective-permute-start(f32[2,2,16384]{2,1,0:T(2,128)S(1)} %convolution_bitcast_fusion.4), channel_id=1, source_target_pairs={{16,0},{24,8},{32,16},{40,24},{48,32},{56,40},{64,48},{72,56},{80,... | collective-permute-start | bytes 786440 | tf_op jit(solution)/shard_map/ppermute | solution.py:15
  113.3 6.5 %collective-permute-start.7 = (f32[2,2,16384]{2,1,0:T(2,128)S(1)}, f32[2,2,16384]{2,1,0:T(2,128)S(1)}, u32[]{:S(2)}, u32[]{:S(2)}) collective-permute-start(f32[2,2,16384]{2,1,0:T(2,128)S(1)} %convolution_bitcast_fusion.3), channel_id=1, source_target_pairs={{32,0},{40,8},{48,16},{56,24},{64,32},{72,40},{80,48},{88,56},{96,... | collective-permute-start | bytes 786440 | tf_op jit(solution)/shard_map/ppermute | solution.py:15
  121.2 1.9 %collective-permute-start.8 = (f32[2,2,16384]{2,1,0:T(2,128)}, f32[2,2,16384]{2,1,0:T(2,128)S(1)}, u32[]{:S(2)}, u32[]{:S(2)}) collective-permute-start(f32[2,2,16384]{2,1,0:T(2,128)} %convolution_bitcast_fusion.2), channel_id=1, source_target_pairs={{64,0},{72,8},{80,16},{88,24},{96,32},{104,40},{112,48},{120,56},{... | collective-permute-start | bytes 786440 | tf_op jit(solution)/shard_map/ppermute | solution.py:15
  127.2 1.9 %collective-permute-start.5 = (f32[2,2,16384]{2,1,0:T(2,128)S(1)}, f32[2,2,16384]{2,1,0:T(2,128)S(1)}, u32[]{:S(2)}, u32[]{:S(2)}) collective-permute-start(f32[2,2,16384]{2,1,0:T(2,128)S(1)} %fusion.4), channel_id=1, source_target_pairs={{8,0},{16,8},{24,16},{32,24},{40,32},{48,40},{56,48},{64,56},{72,6... | collective-permute-start | bytes 786440 | tf_op jit(solution)/shard_map/ppermute | solution.py:15
  131.6 4.5 %collective-permute-done.8 = f32[2,2,16384]{2,1,0:T(2,128)S(1)} collective-permute-done((f32[2,2,16384]{2,1,0:T(2,128)}, f32[2,2,16384]{2,1,0:T(2,128)S(1)}, u32[]{:S(2)}, u32[]{:S(2)}) %collective-permute-start.8) | collective-permute-done | bytes 262176 | tf_op jit(solution)/shard_map/ppermute | solution.py:15
  136.1 5.6 %collective-permute-done.5 = f32[2,2,16384]{2,1,0:T(2,128)S(1)} collective-permute-done((f32[2,2,16384]{2,1,0:T(2,128)S(1)}, f32[2,2,16384]{2,1,0:T(2,128)S(1)}, u32[]{:S(2)}, u32[]{:S(2)}) %collective-permute-start.5) | collective-permute-done | bytes 262176 | tf_op jit(solution)/shard_map/ppermute | solution.py:15
  141.6 1.4 fusion.48
  (185 shorter events, 40.5 us)
Async XLA Ops:
  1.5 51.0 %copy-start.19 = (bf16[32,4096]{1,0:T(8,128)(2,1)S(1)}, bf16[32,4096]{1,0:T(8,128)(2,1)}, u32[]{:S(2)}) copy-start(bf16[32,4096]{1,0:T(8,128)(2,1)} %param.10) | copy-start | bytes 786436
  2.1 14.8 %all-to-all-start = ((bf16[32,8,128]{2,0,1:T(8,128)(2,1)}), bf16[32,8,128]{2,0,1:T(8,128)(2,1)S(1)}, u32[]{:S(2)}, u32[]{:S(2)}) async-start(bf16[32,8,128]{2,0,1:T(8,128)(2,1)} %copy_bitcast_fusion.5), calls=%async_computation | async-start | bytes 131072 | tf_op jit(solution)/shard_map/all_to_all | solution.py:22
  17.0 10.4 %all-to-all-start.1 = ((bf16[32,8,128]{2,0,1:T(8,128)(2,1)}), bf16[32,8,128]{2,0,1:T(8,128)(2,1)S(1)}, u32[]{:S(2)}, u32[]{:S(2)}) async-start(bf16[32,8,128]{2,0,1:T(8,128)(2,1)} %copy_bitcast_fusion.4), calls=%async_computation.1 | async-start | bytes 131072 | tf_op jit(solution)/shard_map/all_to_all | solution.py:23
  27.4 35.8 %all-to-all-start.2 = ((bf16[32,8,512]{2,0,1:T(8,128)(2,1)}), bf16[32,8,512]{2,0,1:T(8,128)(2,1)S(1)}, u32[]{:S(2)}, u32[]{:S(2)}) async-start(bf16[32,8,512]{2,0,1:T(8,128)(2,1)} %bitcast.316), calls=%async_computation.2 | async-start | bytes 524288 | tf_op jit(solution)/shard_map/all_to_all | solution.py:20
  30.8 22.4 %collective-permute-start.4 = (bf16[2,256,128]{2,1,0:T(8,128)(2,1)S(1)}, bf16[2,256,128]{2,1,0:T(8,128)(2,1)S(1)}, u32[]{:S(2)}, u32[]{:S(2)}) collective-permute-start(bf16[2,256,128]{2,1,0:T(8,128)(2,1)S(1)} %pad_maximum_fusion.2), channel_id=1, source_target_pairs={{0,128},{8,136},{16,144},{24,152},{32,160},{40,168},{48,176},{56,1... | collective-permute-start | bytes 393224 | tf_op jit(solution)/shard_map/ppermute | solution.py:15
  34.9 18.9 %collective-permute-start.3 = (bf16[2,256,128]{2,1,0:T(8,128)(2,1)S(1)}, bf16[2,256,128]{2,1,0:T(8,128)(2,1)S(1)}, u32[]{:S(2)}, u32[]{:S(2)}) collective-permute-start(bf16[2,256,128]{2,1,0:T(8,128)(2,1)S(1)} %pad_maximum_fusion.2), channel_id=1, source_target_pairs={{0,64},{8,72},{16,80},{24,88},{32,96},{40,104},{48,112},{56,120},{... | collective-permute-start | bytes 393224 | tf_op jit(solution)/shard_map/ppermute | solution.py:15
  36.8 17.6 %collective-permute-start.2 = (bf16[2,256,128]{2,1,0:T(8,128)(2,1)S(1)}, bf16[2,256,128]{2,1,0:T(8,128)(2,1)S(1)}, u32[]{:S(2)}, u32[]{:S(2)}) collective-permute-start(bf16[2,256,128]{2,1,0:T(8,128)(2,1)S(1)} %pad_maximum_fusion.2), channel_id=1, source_target_pairs={{0,32},{8,40},{16,48},{24,56},{32,64},{40,72},{48,80},{56,88},{64,... | collective-permute-start | bytes 393224 | tf_op jit(solution)/shard_map/ppermute | solution.py:15
  45.9 13.6 %collective-permute-start.1 = (bf16[2,256,128]{2,1,0:T(8,128)(2,1)S(1)}, bf16[2,256,128]{2,1,0:T(8,128)(2,1)S(1)}, u32[]{:S(2)}, u32[]{:S(2)}) collective-permute-start(bf16[2,256,128]{2,1,0:T(8,128)(2,1)S(1)} %pad_maximum_fusion.2), channel_id=1, source_target_pairs={{0,16},{8,24},{16,32},{24,40},{32,48},{40,56},{48,64},{56,72},{64,... | collective-permute-start | bytes 393224 | tf_op jit(solution)/shard_map/ppermute | solution.py:15
  49.3 12.0 %collective-permute-start = (bf16[2,256,128]{2,1,0:T(8,128)(2,1)S(1)}, bf16[2,256,128]{2,1,0:T(8,128)(2,1)S(1)}, u32[]{:S(2)}, u32[]{:S(2)}) collective-permute-start(bf16[2,256,128]{2,1,0:T(8,128)(2,1)S(1)} %pad_maximum_fusion.2), channel_id=1, source_target_pairs={{0,8},{8,16},{16,24},{24,32},{32,40},{40,48},{48,56},{56,64},{64,7... | collective-permute-start | bytes 393224 | tf_op jit(solution)/shard_map/ppermute | solution.py:15
  63.2 12.0 %all-to-all-start.3 = ((bf16[32,8,512]{2,0,1:T(8,128)(2,1)}), bf16[32,8,512]{2,0,1:T(8,128)(2,1)S(1)}, u32[]{:S(2)}, u32[]{:S(2)}) async-start(bf16[32,8,512]{2,0,1:T(8,128)(2,1)} %bitcast.315), calls=%async_computation.3 | async-start | bytes 524288 | tf_op jit(solution)/shard_map/all_to_all | solution.py:21
  76.0 20.1 %copy-start.9 = (bf16[2,128,1,128]{1,3,0,2:T(8,128)(2,1)}, bf16[2,128,1,128]{1,3,0,2:T(8,128)(2,1)S(1)}, u32[]{:S(2)}) copy-start(bf16[2,128,1,128]{1,3,0,2:T(8,128)(2,1)S(1)} %copy.183) | copy-start | bytes 196612
  77.2 9.6 %copy-start.13 = (bf16[2,128,1,128]{3,2,1,0:T(2,128)(2,1)}, bf16[2,128,1,128]{3,2,1,0:T(2,128)(2,1)S(1)}, u32[]{:S(2)}) copy-start(bf16[2,128,1,128]{3,2,1,0:T(2,128)(2,1)S(1)} %get-tuple-element.24) | copy-start | bytes 196612
  78.8 5.5 %copy-start.6 = (f32[2,128,896]{1,2,0:T(8,128)}, f32[2,128,896]{1,2,0:T(8,128)S(1)}, u32[]{:S(2)}) copy-start(f32[2,128,896]{1,2,0:T(8,128)S(1)} %get-tuple-element.44) | copy-start | bytes 2752516
  106.7 5.9 %copy-start.31 = (s32[2]{0:T(128)S(1)}, s32[2]{0:T(128)}, u32[]{:S(2)}) copy-start(s32[2]{0:T(128)} %get-tuple-element.9) | copy-start | bytes 28
  106.7 5.9 %copy-start.35 = (pred[2]{0:T(512)(128)(4,1)S(1)}, pred[2]{0:T(512)(128)(4,1)}, u32[]{:S(2)}) copy-start(pred[2]{0:T(512)(128)(4,1)} %get-tuple-element.40) | copy-start | bytes 10
  107.4 12.4 %copy-start.30 = (s32[2]{0:T(128)S(1)}, s32[2]{0:T(128)}, u32[]{:S(2)}) copy-start(s32[2]{0:T(128)} %get-tuple-element.8) | copy-start | bytes 28
  107.5 12.4 %copy-start.34 = (pred[2]{0:T(512)(128)(4,1)S(1)}, pred[2]{0:T(512)(128)(4,1)}, u32[]{:S(2)}) copy-start(pred[2]{0:T(512)(128)(4,1)} %get-tuple-element.39) | copy-start | bytes 10
  107.5 15.7 %copy-start.29 = (s32[2]{0:T(128)S(1)}, s32[2]{0:T(128)}, u32[]{:S(2)}) copy-start(s32[2]{0:T(128)} %get-tuple-element.7) | copy-start | bytes 28
  107.5 15.7 %copy-start.33 = (pred[2]{0:T(512)(128)(4,1)S(1)}, pred[2]{0:T(512)(128)(4,1)}, u32[]{:S(2)}) copy-start(pred[2]{0:T(512)(128)(4,1)} %get-tuple-element.38) | copy-start | bytes 10
  107.5 18.3 %copy-start.28 = (pred[2]{0:T(512)(128)(4,1)S(1)}, pred[2]{0:T(512)(128)(4,1)}, u32[]{:S(2)}) copy-start(pred[2]{0:T(512)(128)(4,1)} %get-tuple-element.42) | copy-start | bytes 10
  108.3 19.0 %copy-start.1 = (f32[2,2,7,16384]{3,1,0,2:T(2,128)}, f32[2,2,7,16384]{3,1,0,2:T(2,128)S(1)}, u32[]{:S(2)}) copy-start(f32[2,2,7,16384]{3,1,0,2:T(2,128)S(1)} %copy_dynamic-update-slice_fusion) | copy-start | bytes 5505028
  108.9 20.2 %copy-start.3 = (bf16[2,128,896]{1,2,0:T(8,128)(2,1)S(1)}, bf16[2,128,896]{1,2,0:T(8,128)(2,1)}, u32[]{:S(2)}) copy-start(bf16[2,128,896]{1,2,0:T(8,128)(2,1)} %copy-done.2) | copy-start | bytes 1376260
  109.0 22.6 %collective-permute-start.6 = (f32[2,2,16384]{2,1,0:T(2,128)S(1)}, f32[2,2,16384]{2,1,0:T(2,128)S(1)}, u32[]{:S(2)}, u32[]{:S(2)}) collective-permute-start(f32[2,2,16384]{2,1,0:T(2,128)S(1)} %convolution_bitcast_fusion.4), channel_id=1, source_target_pairs={{16,0},{24,8},{32,16},{40,24},{48,32},{56,40},{64,48},{72,56},{80,... | collective-permute-start | bytes 786440 | tf_op jit(solution)/shard_map/ppermute | solution.py:15
  113.3 18.3 %collective-permute-start.7 = (f32[2,2,16384]{2,1,0:T(2,128)S(1)}, f32[2,2,16384]{2,1,0:T(2,128)S(1)}, u32[]{:S(2)}, u32[]{:S(2)}) collective-permute-start(f32[2,2,16384]{2,1,0:T(2,128)S(1)} %convolution_bitcast_fusion.3), channel_id=1, source_target_pairs={{32,0},{40,8},{48,16},{56,24},{64,32},{72,40},{80,48},{88,56},{96,... | collective-permute-start | bytes 786440 | tf_op jit(solution)/shard_map/ppermute | solution.py:15
  119.9 9.7 %copy-start.24 = (bf16[2,128,1,128]{3,1,0,2:T(8,128)(2,1)S(1)}, bf16[2,128,1,128]{3,1,0,2:T(8,128)(2,1)}, u32[]{:S(2)}) copy-start(bf16[2,128,1,128]{3,1,0,2:T(8,128)(2,1)} %fusion.34) | copy-start | bytes 196612
  119.9 9.7 %copy-start.25 = (bf16[2,128,1,128]{3,1,0,2:T(8,128)(2,1)S(1)}, bf16[2,128,1,128]{3,1,0,2:T(8,128)(2,1)}, u32[]{:S(2)}) copy-start(bf16[2,128,1,128]{3,1,0,2:T(8,128)(2,1)} %fusion.35) | copy-start | bytes 196612
  119.9 9.7 %copy-start.26 = (bf16[2,128,1,128]{3,1,0,2:T(8,128)(2,1)S(1)}, bf16[2,128,1,128]{3,1,0,2:T(8,128)(2,1)}, u32[]{:S(2)}) copy-start(bf16[2,128,1,128]{3,1,0,2:T(8,128)(2,1)} %fusion.36) | copy-start | bytes 196612
  121.2 14.8 %collective-permute-start.8 = (f32[2,2,16384]{2,1,0:T(2,128)}, f32[2,2,16384]{2,1,0:T(2,128)S(1)}, u32[]{:S(2)}, u32[]{:S(2)}) collective-permute-start(f32[2,2,16384]{2,1,0:T(2,128)} %convolution_bitcast_fusion.2), channel_id=1, source_target_pairs={{64,0},{72,8},{80,16},{88,24},{96,32},{104,40},{112,48},{120,56},{... | collective-permute-start | bytes 786440 | tf_op jit(solution)/shard_map/ppermute | solution.py:15
  124.5 11.5 %collective-permute-start.9 = (f32[2,2,16384]{2,1,0:T(2,128)}, f32[2,2,16384]{2,1,0:T(2,128)S(1)}, u32[]{:S(2)}, u32[]{:S(2)}) collective-permute-start(f32[2,2,16384]{2,1,0:T(2,128)} %convolution_bitcast_fusion.1), channel_id=1, source_target_pairs={{128,0},{136,8},{144,16},{152,24},{160,32},{168,40},{176,48},{184,... | collective-permute-start | bytes 786440 | tf_op jit(solution)/shard_map/ppermute | solution.py:15
  126.5 4.0 %copy-start.20 = (bf16[2,128,1,128]{1,3,0,2:T(8,128)(2,1)S(1)}, bf16[2,128,1,128]{1,3,0,2:T(8,128)(2,1)}, u32[]{:S(2)}) copy-start(bf16[2,128,1,128]{1,3,0,2:T(8,128)(2,1)} %get-tuple-element.30) | copy-start | bytes 196612
  126.5 4.0 %copy-start.21 = (bf16[2,128,1,128]{1,3,0,2:T(8,128)(2,1)S(1)}, bf16[2,128,1,128]{1,3,0,2:T(8,128)(2,1)}, u32[]{:S(2)}) copy-start(bf16[2,128,1,128]{1,3,0,2:T(8,128)(2,1)} %get-tuple-element.36) | copy-start | bytes 196612
  127.2 14.4 %collective-permute-start.5 = (f32[2,2,16384]{2,1,0:T(2,128)S(1)}, f32[2,2,16384]{2,1,0:T(2,128)S(1)}, u32[]{:S(2)}, u32[]{:S(2)}) collective-permute-start(f32[2,2,16384]{2,1,0:T(2,128)S(1)} %fusion.4), channel_id=1, source_target_pairs={{8,0},{16,8},{24,16},{32,24},{40,32},{48,40},{56,48},{64,56},{72,6... | collective-permute-start | bytes 786440 | tf_op jit(solution)/shard_map/ppermute | solution.py:15
  (23 other events, 46.2 us)
where the time goes:
time: 146 us; the launch traced here: 145 us
  starting transfers between devices  53.8 us (37%)
  waiting for transfers between devices  28.8 us (20%)
  matrix products  28 us (19%)
  local copies, waits for them, and re-layouts  23.6 us (16%)
  other arithmetic  8.61 us (6%)
  between operations  1.62 us (1%)
    ppermute x10, starting transfers between devices, from_behind(): lax.ppermute(value, axis, [(source, source + steps) for source in range(i...  36.7 us
    ppermute x10, waiting for transfers between devices, from_behind(): lax.ppermute(value, axis, [(source, source + steps) for source in range(i...  15.9 us
    all_to_all x1, waiting for transfers between devices, shards(): lax.all_to_all(output_gradient, 'head', split_axis=1, concat_axis=0, tile...  7.33 us
    sub x4, matrix products, shards(): exp_scores = jnp.exp(scores - row_max)  6.54 us
    all_to_all x1, waiting for transfers between devices, shards(): lax.all_to_all(value_projection, 'head', split_axis=1, concat_axis=0, til...  5.61 us
    unnamed x90, local copies, waits for them, and re-layouts  5.56 us
    all_to_all x1, starting transfers between devices, shards(): lax.all_to_all(value_projection, 'head', split_axis=1, concat_axis=0, til...  4.81 us
    dot_general x5, matrix products, shards(): jnp.einsum('qp,sqx->spx', one_hot, grads[:, :, 1 + column], precision=hig...  4.59 us
  transfers between devices with their start and end apart: 14, of which 6 were waited for; matrix products, arithmetic and copies ran while one was open for 16% of the time, Pallas kernels for 0%

commit v1 on v0

--- a/solution.py
+++ b/solution.py
@@ -1,3 +1,4 @@
+import functools
 import math
 import jax
 import jax.numpy as jnp
@@ -7,6 +8,27 @@
 HEAD_SIZE = 128
 BLOCK_TOKENS = 128
 masked_score = -1e30
+
+
+def change_yards_on(chunk, row_axis):
+    long_array = lax.axis_size(row_axis)
+    part_now, val = (long_array, lax.axis_index(row_axis))
+    kept_arr = chunk.shape[1] // part_now
+    v_now = list(chunk.shape)
+    v_now[1] = kept_arr
+    val2 = v_now[0]
+    v_now[0] = val2 * part_now
+    x_now = jnp.zeros(v_now, chunk.dtype)
+    for d in range(part_now):
+        mid_arr = lax.dynamic_slice_in_dim(chunk, (val ^ d) * kept_arr, kept_arr, axis=1)
+        if d:
+            outer = tuple(((k0, k0 ^ d) for k0 in range(part_now)))
+            mid_arr = lax.ppermute(mid_arr, axis_name=row_axis, perm=outer)
+        x_now = lax.dynamic_update_slice_in_dim(x_now, mid_arr, (val ^ d) * val2, axis=0)
+    return x_now
+
+
+resolve_vectors = functools.partial(change_yards_on, row_axis="head")
 
 
 def from_behind(value, axis, steps):
@@ -19,7 +41,7 @@
     q_local, dout_local, k_local, v_local = (
         lax.all_to_all(query_projection, "head", split_axis=1, concat_axis=0, tiled=True),
         lax.all_to_all(output_gradient, "head", split_axis=1, concat_axis=0, tiled=True),
-        lax.all_to_all(key_projection, "head", split_axis=1, concat_axis=0, tiled=True),
+        resolve_vectors(key_projection),
         lax.all_to_all(value_projection, "head", split_axis=1, concat_axis=0, tiled=True),
     )
     tokens_dev = q_local.shape[0]

time: 146 us -> 150 us (1.027)
  starting transfers between devices: 53.8 us -> 60.6 us
  waiting for transfers between devices: 28.8 us -> 26.7 us
    ppermute x0 -> x7, starting transfers between devices: none -> 11.6 us  [change_yards_on(): mid_arr = lax.ppermute(mid_arr, axis_name=row_axis, perm=outer)]
    all_to_all x1, waiting for transfers between devices: 5.61 us -> 0.01 us  [shards(): lax.all_to_all(value_projection, 'head', split_axis=1, concat_axis=0, til...]
    all_to_all x1 -> x0, starting transfers between devices: 4.47 us -> none  [shards(): lax.all_to_all(key_projection, 'head', split_axis=1, concat_axis=0, tiled...]
    ppermute x0 -> x7, waiting for transfers between devices: none -> 3.42 us  [change_yards_on(): mid_arr = lax.ppermute(mid_arr, axis_name=row_axis, perm=outer)]
  transfers between devices with their start and end apart: 14 -> 20, of which waited for: 6 -> 7; matrix products, arithmetic and copies ran while one was open for 16% -> 15% of each run, Pallas kernels for 0% -> 0%
where the time goes in v1:
time: 150 us; the launch traced here: 149 us
  starting transfers between devices  60.6 us (40%)
  matrix products  28 us (19%)
  waiting for transfers between devices  26.7 us (18%)
  local copies, waits for them, and re-layouts  23 us (15%)
  other arithmetic  8.67 us (6%)
  between operations  1.7 us (1%)
    ppermute x10, starting transfers between devices, from_behind(): lax.ppermute(value, axis, [(source, source + steps) for source in range(i...  36.7 us
    ppermute x10, waiting for transfers between devices, from_behind(): lax.ppermute(value, axis, [(source, source + steps) for source in range(i...  15.9 us
    ppermute x7, starting transfers between devices, change_yards_on(): mid_arr = lax.ppermute(mid_arr, axis_name=row_axis, perm=outer)  11.6 us
    all_to_all x1, waiting for transfers between devices, shards(): lax.all_to_all(output_gradient, 'head', split_axis=1, concat_axis=0, tile...  7.33 us
    sub x4, matrix products, shards(): exp_scores = jnp.exp(scores - row_max)  6.57 us
    unnamed x90, local copies, waits for them, and re-layouts  4.73 us
    dot_general x5, matrix products, shards(): jnp.einsum('qp,sqx->spx', one_hot, grads[:, :, 1 + column], precision=hig...  4.62 us
    all_to_all x1, starting transfers between devices, shards(): lax.all_to_all(output_gradient, 'head', split_axis=1, concat_axis=0, tile...  4.46 us
  transfers between devices with their start and end apart: 20, of which 7 were waited for; matrix products, arithmetic and copies ran while one was open for 15% of the time, Pallas kernels for 0%

profile of v1, /device:TPU:2, one launch (start us, length us, event | category | flops | bytes accessed | tf_op | source)
XLA Modules:
  0.0 148.6 jit_solution(2785733351482692148)
XLA Ops:
  1.6 2.5 %collective-permute-start.6 = (bf16[32,128]{1,0:T(8,128)(2,1)S(1)}, bf16[32,128]{1,0:T(8,128)(2,1)S(1)}, u32[]{:S(2)}, u32[]{:S(2)}) collective-permute-start(bf16[32,128]{1,0:T(8,128)(2,1)S(1)} %get-tuple-element.37), channel_id=1, source_target_pairs={{0,7},{1,6},{2,5},{3,4},{4,3},{5,2},{6,1},{7,0},{8,15},{9,14},{10,... | collective-permute-start | bytes 24584 | tf_op jit(solution)/shard_map/ppermute | solution.py:26
  5.0 2.9 %collective-permute-start.3 = (bf16[32,128]{1,0:T(8,128)(2,1)S(1)}, bf16[32,128]{1,0:T(8,128)(2,1)S(1)}, u32[]{:S(2)}, u32[]{:S(2)}) collective-permute-start(bf16[32,128]{1,0:T(8,128)(2,1)S(1)} %get-tuple-element.39), channel_id=1, source_target_pairs={{0,4},{1,5},{2,6},{3,7},{4,0},{5,1},{6,2},{7,3},{8,12},{9,13},{10,... | collective-permute-start | bytes 24584 | tf_op jit(solution)/shard_map/ppermute | solution.py:26
  8.8 3.4 %all-to-all-start = ((bf16[32,8,128]{2,0,1:T(8,128)(2,1)}), bf16[32,8,128]{2,0,1:T(8,128)(2,1)S(1)}, u32[]{:S(2)}, u32[]{:S(2)}) async-start(bf16[32,8,128]{2,0,1:T(8,128)(2,1)} %copy_bitcast_fusion.4), calls=%async_computation | async-start | bytes 131072 | tf_op jit(solution)/shard_map/all_to_all | solution.py:45
  12.9 1.8 %fusion.95 = (s32[2]{0:T(128)S(1)}, s32[2]{0:T(128)S(1)}, s32[2]{0:T(128)}, s32[2]{0:T(128)}, s32[2]{0:T(128)}, /*index=5*/s32[2]{0:T(128)}, s32[2]{0:T(128)S(1)...) fusion(s32[2,6]{1,0:T(2,128)} %param.11, s32[]{:T(128)S(6)} %sub.154, ...), kind=kLoop, calls=%fused_computation.235 | loop fusion | flops 32 | bytes 168 | tf_op jit(solution)/shard_map/sub | solution.py:71
  17.1 2.2 %gather_fusion = pred[896,2]{1,0:T(8,128)(4,1)S(1)} fusion(pred[2,7]{0,1:T(8,128)(4,1)S(1)} %concatenate.9, s32[1024]{0:T(1024)S(1)} %pad_clamp_fusion.6), kind=kCustom, calls=%fused_computation.5 | custom fusion | bytes 7168 | tf_op jit(solution)/shard_map/gather | solution.py:86
  20.2 1.7 %copy.224 = bf16[4,8,8,512]{3,2,0,1:T(8,128)(2,1)} copy(bf16[4,8,8,512]{3,2,1,0:T(8,128)(2,1)} %bitcast.350) | data formatting | bytes 524288 | tf_op jit(solution)/shard_map/all_to_all | solution.py:42
  21.8 1.9 %collective-permute-start.1 = (bf16[32,128]{1,0:T(8,128)(2,1)S(1)}, bf16[32,128]{1,0:T(8,128)(2,1)S(1)}, u32[]{:S(2)}, u32[]{:S(2)}) collective-permute-start(bf16[32,128]{1,0:T(8,128)(2,1)S(1)} %get-tuple-element.41), channel_id=1, source_target_pairs={{0,2},{1,3},{2,0},{3,1},{4,6},{5,7},{6,4},{7,5},{8,10},{9,11},{10,... | collective-permute-start | bytes 24584 | tf_op jit(solution)/shard_map/ppermute | solution.py:26
  23.8 1.8 %collective-permute-done.1 = bf16[32,128]{1,0:T(8,128)(2,1)S(1)} collective-permute-done((bf16[32,128]{1,0:T(8,128)(2,1)S(1)}, bf16[32,128]{1,0:T(8,128)(2,1)S(1)}, u32[]{:S(2)}, u32[]{:S(2)}) %collective-permute-start.1) | collective-permute-done | bytes 8224 | tf_op jit(solution)/shard_map/ppermute | solution.py:26
  25.5 3.1 %collective-permute-start.5 = (bf16[32,128]{1,0:T(8,128)(2,1)S(1)}, bf16[32,128]{1,0:T(8,128)(2,1)S(1)}, u32[]{:S(2)}, u32[]{:S(2)}) collective-permute-start(bf16[32,128]{1,0:T(8,128)(2,1)S(1)} %get-tuple-element.43), channel_id=1, source_target_pairs={{0,6},{1,7},{2,4},{3,5},{4,2},{5,3},{6,0},{7,1},{8,14},{9,15},{10,... | collective-permute-start | bytes 24584 | tf_op jit(solution)/shard_map/ppermute | solution.py:26
  28.7 1.7 %collective-permute-done.5 = bf16[32,128]{1,0:T(8,128)(2,1)S(1)} collective-permute-done((bf16[32,128]{1,0:T(8,128)(2,1)S(1)}, bf16[32,128]{1,0:T(8,128)(2,1)S(1)}, u32[]{:S(2)}, u32[]{:S(2)}) %collective-permute-start.5) | collective-permute-done | bytes 8224 | tf_op jit(solution)/shard_map/ppermute | solution.py:26
  30.4 4.4 %all-to-all-start.1 = ((bf16[32,8,512]{2,0,1:T(8,128)(2,1)}), bf16[32,8,512]{2,0,1:T(8,128)(2,1)S(1)}, u32[]{:S(2)}, u32[]{:S(2)}) async-start(bf16[32,8,512]{2,0,1:T(8,128)(2,1)} %bitcast.322), calls=%async_computation.1 | async-start | bytes 524288 | tf_op jit(solution)/shard_map/all_to_all | solution.py:42
  34.9 4.0 %collective-permute-start.11 = (bf16[2,256,128]{2,1,0:T(8,128)(2,1)S(1)}, bf16[2,256,128]{2,1,0:T(8,128)(2,1)S(1)}, u32[]{:S(2)}, u32[]{:S(2)}) collective-permute-start(bf16[2,256,128]{2,1,0:T(8,128)(2,1)S(1)} %pad_maximum_fusion.2), channel_id=1, source_target_pairs={{0,128},{8,136},{16,144},{24,152},{32,160},{40,168},{48,176},{56,1... | collective-permute-start | bytes 393224 | tf_op jit(solution)/shard_map/ppermute | solution.py:37
  38.9 1.9 %collective-permute-start.10 = (bf16[2,256,128]{2,1,0:T(8,128)(2,1)S(1)}, bf16[2,256,128]{2,1,0:T(8,128)(2,1)S(1)}, u32[]{:S(2)}, u32[]{:S(2)}) collective-permute-start(bf16[2,256,128]{2,1,0:T(8,128)(2,1)S(1)} %pad_maximum_fusion.2), channel_id=1, source_target_pairs={{0,64},{8,72},{16,80},{24,88},{32,96},{40,104},{48,112},{56,120},{... | collective-permute-start | bytes 393224 | tf_op jit(solution)/shard_map/ppermute | solution.py:37
  40.8 9.1 %collective-permute-start.9 = (bf16[2,256,128]{2,1,0:T(8,128)(2,1)S(1)}, bf16[2,256,128]{2,1,0:T(8,128)(2,1)S(1)}, u32[]{:S(2)}, u32[]{:S(2)}) collective-permute-start(bf16[2,256,128]{2,1,0:T(8,128)(2,1)S(1)} %pad_maximum_fusion.2), channel_id=1, source_target_pairs={{0,32},{8,40},{16,48},{24,56},{32,64},{40,72},{48,80},{56,88},{64,... | collective-permute-start | bytes 393224 | tf_op jit(solution)/shard_map/ppermute | solution.py:37
  49.9 3.4 %collective-permute-start.8 = (bf16[2,256,128]{2,1,0:T(8,128)(2,1)S(1)}, bf16[2,256,128]{2,1,0:T(8,128)(2,1)S(1)}, u32[]{:S(2)}, u32[]{:S(2)}) collective-permute-start(bf16[2,256,128]{2,1,0:T(8,128)(2,1)S(1)} %pad_maximum_fusion.2), channel_id=1, source_target_pairs={{0,16},{8,24},{16,32},{24,40},{32,48},{40,56},{48,64},{56,72},{64,... | collective-permute-start | bytes 393224 | tf_op jit(solution)/shard_map/ppermute | solution.py:37
  53.3 2.9 %collective-permute-start.7 = (bf16[2,256,128]{2,1,0:T(8,128)(2,1)S(1)}, bf16[2,256,128]{2,1,0:T(8,128)(2,1)S(1)}, u32[]{:S(2)}, u32[]{:S(2)}) collective-permute-start(bf16[2,256,128]{2,1,0:T(8,128)(2,1)S(1)} %pad_maximum_fusion.2), channel_id=1, source_target_pairs={{0,8},{8,16},{16,24},{24,32},{32,40},{40,48},{48,56},{56,64},{64,7... | collective-permute-start | bytes 393224 | tf_op jit(solution)/shard_map/ppermute | solution.py:37
  59.0 4.7 %collective-permute-done.8 = bf16[2,256,128]{2,1,0:T(8,128)(2,1)S(1)} collective-permute-done((bf16[2,256,128]{2,1,0:T(8,128)(2,1)S(1)}, bf16[2,256,128]{2,1,0:T(8,128)(2,1)S(1)}, u32[]{:S(2)}, u32[]{:S(2)}) %collective-permute-start.8) | collective-permute-done | bytes 131104 | tf_op jit(solution)/shard_map/ppermute | solution.py:37
  67.3 4.5 %all-to-all-start.2 = ((bf16[32,8,512]{2,0,1:T(8,128)(2,1)}), bf16[32,8,512]{2,0,1:T(8,128)(2,1)S(1)}, u32[]{:S(2)}, u32[]{:S(2)}) async-start(bf16[32,8,512]{2,0,1:T(8,128)(2,1)} %bitcast.321), calls=%async_computation.2 | async-start | bytes 524288 | tf_op jit(solution)/shard_map/all_to_all | solution.py:43
  72.0 7.3 %all-to-all-done.2 = bf16[32,8,512]{2,0,1:T(8,128)(2,1)S(1)} async-done(((bf16[32,8,512]{2,0,1:T(8,128)(2,1)}), bf16[32,8,512]{2,0,1:T(8,128)(2,1)S(1)}, u32[]{:S(2)}, u32[]{:S(2)}) %all-to-all-start.2) | async-done | bytes 262176 | tf_op jit(solution)/shard_map/all_to_all | solution.py:43
  81.4 1.6 %fusion.125 = (f32[2,128]{1,0:T(2,128)S(1)}, f32[2,128,896]{1,2,0:T(8,128)S(1)}) fusion(bf16[2,896,128]{2,1,0:T(8,128)(2,1)S(1)} %bitcast.331, pred[2,896]{1,0:T(4,128)(4,1)S(1)} %copy.115, pred[128,896]{0,1:T(8,128)(4,1)} %fusion.38, bf16[2,128,1,128]{3,2,1,0:T(2,128)(2,1)S(1)} %get-tuple-element.26), kind=kOutput, calls=%fused_computation.265 | convolution fusion | flops 59868032 | bytes 1559296 | tf_op jit(solution)/shard_map/sub | solution.py:103
  82.9 1.6 %fusion.128 = (f32[2,128]{1,0:T(2,128)S(1)}, f32[2,128,896]{1,2,0:T(8,128)S(1)}) fusion(bf16[2,896,128]{2,1,0:T(8,128)(2,1)S(1)} %bitcast.332, pred[2,896]{1,0:T(4,128)(4,1)S(1)} %copy.115, pred[128,896]{0,1:T(8,128)(4,1)} %fusion.38, bf16[2,128,1,128]{3,2,1,0:T(2,128)(2,1)S(1)} %get-tuple-element.23), kind=kOutput, calls=%fused_computation.268 | convolution fusion | flops 59868032 | bytes 1559296 | tf_op jit(solution)/shard_map/sub | solution.py:103
  85.8 1.5 %multiply_reduce_fusion.3 = (f32[2,128]{1,0:T(2,128)}, bf16[2,128,1,128]{1,3,0,2:T(8,128)(2,1)}) fusion(bf16[2,128,1,128]{1,3,0,2:T(8,128)(2,1)S(1)} %copy.177, bf16[2,128,896]{1,2,0:T(8,128)(2,1)S(1)} %fusion.39, bf16[2,896,128]{2,1,0:T(8,128)(2,1)S(1)} %bitcast.323), kind=kOutput, calls=%fused_computation.119 | convolution fusion | flops 58851072 | bytes 1049600 | tf_op jit(solution)/shard_map/awv,avq->awq/dot_general | solution.py:106
  88.4 1.5 fusion.29
  90.9 1.4 fusion.126
  95.9 2.0 %fusion.127 = (f32[2,128]{1,0:T(2,128)}, f32[2,128,896]{1,2,0:T(8,128)}) fusion(bf16[2,896,128]{2,1,0:T(8,128)(2,1)S(1)} %bitcast.336, pred[2,896]{1,0:T(4,128)(4,1)S(1)} %copy.115, pred[128,896]{0,1:T(8,128)(4,1)S(1)} %copy-done.27, bf16[2,128,1,128]{3,2,1,0:T(2,128)(2,1)S(1)} %copy-done.15), kind=kOutput, calls=%fused_computation.267 | convolution fusion | flops 59868032 | bytes 1559296 | tf_op jit(solution)/shard_map/sub | solution.py:103
  106.4 1.5 convolution_add_fusion.2
  113.0 3.7 %collective-permute-start.13 = (f32[2,2,16384]{2,1,0:T(2,128)S(1)}, f32[2,2,16384]{2,1,0:T(2,128)S(1)}, u32[]{:S(2)}, u32[]{:S(2)}) collective-permute-start(f32[2,2,16384]{2,1,0:T(2,128)S(1)} %convolution_bitcast_fusion.4), channel_id=1, source_target_pairs={{16,0},{24,8},{32,16},{40,24},{48,32},{56,40},{64,48},{72,56},{80,... | collective-permute-start | bytes 786440 | tf_op jit(solution)/shard_map/ppermute | solution.py:37
  117.4 6.5 %collective-permute-start.14 = (f32[2,2,16384]{2,1,0:T(2,128)S(1)}, f32[2,2,16384]{2,1,0:T(2,128)S(1)}, u32[]{:S(2)}, u32[]{:S(2)}) collective-permute-start(f32[2,2,16384]{2,1,0:T(2,128)S(1)} %convolution_bitcast_fusion.3), channel_id=1, source_target_pairs={{32,0},{40,8},{48,16},{56,24},{64,32},{72,40},{80,48},{88,56},{96,... | collective-permute-start | bytes 786440 | tf_op jit(solution)/shard_map/ppermute | solution.py:37
  125.3 1.9 %collective-permute-start.15 = (f32[2,2,16384]{2,1,0:T(2,128)}, f32[2,2,16384]{2,1,0:T(2,128)S(1)}, u32[]{:S(2)}, u32[]{:S(2)}) collective-permute-start(f32[2,2,16384]{2,1,0:T(2,128)} %convolution_bitcast_fusion.2), channel_id=1, source_target_pairs={{64,0},{72,8},{80,16},{88,24},{96,32},{104,40},{112,48},{120,56},{... | collective-permute-start | bytes 786440 | tf_op jit(solution)/shard_map/ppermute | solution.py:37
  131.3 1.9 %collective-permute-start.12 = (f32[2,2,16384]{2,1,0:T(2,128)S(1)}, f32[2,2,16384]{2,1,0:T(2,128)S(1)}, u32[]{:S(2)}, u32[]{:S(2)}) collective-permute-start(f32[2,2,16384]{2,1,0:T(2,128)S(1)} %fusion.4), channel_id=1, source_target_pairs={{8,0},{16,8},{24,16},{32,24},{40,32},{48,40},{56,48},{64,56},{72,6... | collective-permute-start | bytes 786440 | tf_op jit(solution)/shard_map/ppermute | solution.py:37
  135.6 4.5 %collective-permute-done.15 = f32[2,2,16384]{2,1,0:T(2,128)S(1)} collective-permute-done((f32[2,2,16384]{2,1,0:T(2,128)}, f32[2,2,16384]{2,1,0:T(2,128)S(1)}, u32[]{:S(2)}, u32[]{:S(2)}) %collective-permute-start.15) | collective-permute-done | bytes 262176 | tf_op jit(solution)/shard_map/ppermute | solution.py:37
  140.2 5.5 %collective-permute-done.12 = f32[2,2,16384]{2,1,0:T(2,128)S(1)} collective-permute-done((f32[2,2,16384]{2,1,0:T(2,128)S(1)}, f32[2,2,16384]{2,1,0:T(2,128)S(1)}, u32[]{:S(2)}, u32[]{:S(2)}) %collective-permute-start.12) | collective-permute-done | bytes 262176 | tf_op jit(solution)/shard_map/ppermute | solution.py:37
  (206 shorter events, 46.7 us)
Async XLA Ops:
  0.6 55.8 %copy-start.19 = (bf16[32,4096]{1,0:T(8,128)(2,1)S(1)}, bf16[32,4096]{1,0:T(8,128)(2,1)}, u32[]{:S(2)}) copy-start(bf16[32,4096]{1,0:T(8,128)(2,1)} %param.10) | copy-start | bytes 786436
  1.6 28.8 %collective-permute-start.6 = (bf16[32,128]{1,0:T(8,128)(2,1)S(1)}, bf16[32,128]{1,0:T(8,128)(2,1)S(1)}, u32[]{:S(2)}, u32[]{:S(2)}) collective-permute-start(bf16[32,128]{1,0:T(8,128)(2,1)S(1)} %get-tuple-element.37), channel_id=1, source_target_pairs={{0,7},{1,6},{2,5},{3,4},{4,3},{5,2},{6,1},{7,0},{8,15},{9,14},{10,... | collective-permute-start | bytes 24584 | tf_op jit(solution)/shard_map/ppermute | solution.py:26
  4.1 24.7 %collective-permute-start.4 = (bf16[32,128]{1,0:T(8,128)(2,1)S(1)}, bf16[32,128]{1,0:T(8,128)(2,1)S(1)}, u32[]{:S(2)}, u32[]{:S(2)}) collective-permute-start(bf16[32,128]{1,0:T(8,128)(2,1)S(1)} %get-tuple-element.38), channel_id=1, source_target_pairs={{0,5},{1,4},{2,7},{3,6},{4,1},{5,0},{6,3},{7,2},{8,13},{9,12},{10,... | collective-permute-start | bytes 24584 | tf_op jit(solution)/shard_map/ppermute | solution.py:26
  5.0 23.7 %collective-permute-start.3 = (bf16[32,128]{1,0:T(8,128)(2,1)S(1)}, bf16[32,128]{1,0:T(8,128)(2,1)S(1)}, u32[]{:S(2)}, u32[]{:S(2)}) collective-permute-start(bf16[32,128]{1,0:T(8,128)(2,1)S(1)} %get-tuple-element.39), channel_id=1, source_target_pairs={{0,4},{1,5},{2,6},{3,7},{4,0},{5,1},{6,2},{7,3},{8,12},{9,13},{10,... | collective-permute-start | bytes 24584 | tf_op jit(solution)/shard_map/ppermute | solution.py:26
  7.9 20.8 %collective-permute-start.2 = (bf16[32,128]{1,0:T(8,128)(2,1)S(1)}, bf16[32,128]{1,0:T(8,128)(2,1)S(1)}, u32[]{:S(2)}, u32[]{:S(2)}) collective-permute-start(bf16[32,128]{1,0:T(8,128)(2,1)S(1)} %get-tuple-element.40), channel_id=1, source_target_pairs={{0,3},{1,2},{2,1},{3,0},{4,7},{5,6},{6,5},{7,4},{8,11},{9,10},{10,... | collective-permute-start | bytes 24584 | tf_op jit(solution)/shard_map/ppermute | solution.py:26
  7.9 14.0 %collective-permute-start = (bf16[32,128]{1,0:T(8,128)(2,1)S(1)}, bf16[32,128]{1,0:T(8,128)(2,1)S(1)}, u32[]{:S(2)}, u32[]{:S(2)}) collective-permute-start(bf16[32,128]{1,0:T(8,128)(2,1)S(1)} %get-tuple-element.42), channel_id=1, source_target_pairs={{0,1},{1,0},{2,3},{3,2},{4,5},{5,4},{6,7},{7,6},{8,9},{9,8},{10,11... | collective-permute-start | bytes 24584 | tf_op jit(solution)/shard_map/ppermute | solution.py:26
  8.8 21.6 %all-to-all-start = ((bf16[32,8,128]{2,0,1:T(8,128)(2,1)}), bf16[32,8,128]{2,0,1:T(8,128)(2,1)S(1)}, u32[]{:S(2)}, u32[]{:S(2)}) async-start(bf16[32,8,128]{2,0,1:T(8,128)(2,1)} %copy_bitcast_fusion.4), calls=%async_computation | async-start | bytes 131072 | tf_op jit(solution)/shard_map/all_to_all | solution.py:45
  21.8 3.7 %collective-permute-start.1 = (bf16[32,128]{1,0:T(8,128)(2,1)S(1)}, bf16[32,128]{1,0:T(8,128)(2,1)S(1)}, u32[]{:S(2)}, u32[]{:S(2)}) collective-permute-start(bf16[32,128]{1,0:T(8,128)(2,1)S(1)} %get-tuple-element.41), channel_id=1, source_target_pairs={{0,2},{1,3},{2,0},{3,1},{4,6},{5,7},{6,4},{7,5},{8,10},{9,11},{10,... | collective-permute-start | bytes 24584 | tf_op jit(solution)/shard_map/ppermute | solution.py:26
  25.5 4.9 %collective-permute-start.5 = (bf16[32,128]{1,0:T(8,128)(2,1)S(1)}, bf16[32,128]{1,0:T(8,128)(2,1)S(1)}, u32[]{:S(2)}, u32[]{:S(2)}) collective-permute-start(bf16[32,128]{1,0:T(8,128)(2,1)S(1)} %get-tuple-element.43), channel_id=1, source_target_pairs={{0,6},{1,7},{2,4},{3,5},{4,2},{5,3},{6,0},{7,1},{8,14},{9,15},{10,... | collective-permute-start | bytes 24584 | tf_op jit(solution)/shard_map/ppermute | solution.py:26
  30.4 36.9 %all-to-all-start.1 = ((bf16[32,8,512]{2,0,1:T(8,128)(2,1)}), bf16[32,8,512]{2,0,1:T(8,128)(2,1)S(1)}, u32[]{:S(2)}, u32[]{:S(2)}) async-start(bf16[32,8,512]{2,0,1:T(8,128)(2,1)} %bitcast.322), calls=%async_computation.1 | async-start | bytes 524288 | tf_op jit(solution)/shard_map/all_to_all | solution.py:42
  34.9 22.4 %collective-permute-start.11 = (bf16[2,256,128]{2,1,0:T(8,128)(2,1)S(1)}, bf16[2,256,128]{2,1,0:T(8,128)(2,1)S(1)}, u32[]{:S(2)}, u32[]{:S(2)}) collective-permute-start(bf16[2,256,128]{2,1,0:T(8,128)(2,1)S(1)} %pad_maximum_fusion.2), channel_id=1, source_target_pairs={{0,128},{8,136},{16,144},{24,152},{32,160},{40,168},{48,176},{56,1... | collective-permute-start | bytes 393224 | tf_op jit(solution)/shard_map/ppermute | solution.py:37
  38.9 18.9 %collective-permute-start.10 = (bf16[2,256,128]{2,1,0:T(8,128)(2,1)S(1)}, bf16[2,256,128]{2,1,0:T(8,128)(2,1)S(1)}, u32[]{:S(2)}, u32[]{:S(2)}) collective-permute-start(bf16[2,256,128]{2,1,0:T(8,128)(2,1)S(1)} %pad_maximum_fusion.2), channel_id=1, source_target_pairs={{0,64},{8,72},{16,80},{24,88},{32,96},{40,104},{48,112},{56,120},{... | collective-permute-start | bytes 393224 | tf_op jit(solution)/shard_map/ppermute | solution.py:37
  40.8 17.6 %collective-permute-start.9 = (bf16[2,256,128]{2,1,0:T(8,128)(2,1)S(1)}, bf16[2,256,128]{2,1,0:T(8,128)(2,1)S(1)}, u32[]{:S(2)}, u32[]{:S(2)}) collective-permute-start(bf16[2,256,128]{2,1,0:T(8,128)(2,1)S(1)} %pad_maximum_fusion.2), channel_id=1, source_target_pairs={{0,32},{8,40},{16,48},{24,56},{32,64},{40,72},{48,80},{56,88},{64,... | collective-permute-start | bytes 393224 | tf_op jit(solution)/shard_map/ppermute | solution.py:37
  49.9 13.7 %collective-permute-start.8 = (bf16[2,256,128]{2,1,0:T(8,128)(2,1)S(1)}, bf16[2,256,128]{2,1,0:T(8,128)(2,1)S(1)}, u32[]{:S(2)}, u32[]{:S(2)}) collective-permute-start(bf16[2,256,128]{2,1,0:T(8,128)(2,1)S(1)} %pad_maximum_fusion.2), channel_id=1, source_target_pairs={{0,16},{8,24},{16,32},{24,40},{32,48},{40,56},{48,64},{56,72},{64,... | collective-permute-start | bytes 393224 | tf_op jit(solution)/shard_map/ppermute | solution.py:37
  53.3 12.1 %collective-permute-start.7 = (bf16[2,256,128]{2,1,0:T(8,128)(2,1)S(1)}, bf16[2,256,128]{2,1,0:T(8,128)(2,1)S(1)}, u32[]{:S(2)}, u32[]{:S(2)}) collective-permute-start(bf16[2,256,128]{2,1,0:T(8,128)(2,1)S(1)} %pad_maximum_fusion.2), channel_id=1, source_target_pairs={{0,8},{8,16},{16,24},{24,32},{32,40},{40,48},{48,56},{56,64},{64,7... | collective-permute-start | bytes 393224 | tf_op jit(solution)/shard_map/ppermute | solution.py:37
  67.3 12.0 %all-to-all-start.2 = ((bf16[32,8,512]{2,0,1:T(8,128)(2,1)}), bf16[32,8,512]{2,0,1:T(8,128)(2,1)S(1)}, u32[]{:S(2)}, u32[]{:S(2)}) async-start(bf16[32,8,512]{2,0,1:T(8,128)(2,1)} %bitcast.321), calls=%async_computation.2 | async-start | bytes 524288 | tf_op jit(solution)/shard_map/all_to_all | solution.py:43
  80.2 20.0 %copy-start.9 = (bf16[2,128,1,128]{1,3,0,2:T(8,128)(2,1)}, bf16[2,128,1,128]{1,3,0,2:T(8,128)(2,1)S(1)}, u32[]{:S(2)}) copy-start(bf16[2,128,1,128]{1,3,0,2:T(8,128)(2,1)S(1)} %copy.178) | copy-start | bytes 196612
  111.5 12.4 %copy-start.30 = (s32[2]{0:T(128)S(1)}, s32[2]{0:T(128)}, u32[]{:S(2)}) copy-start(s32[2]{0:T(128)} %get-tuple-element.8) | copy-start | bytes 28
  111.5 12.4 %copy-start.34 = (pred[2]{0:T(512)(128)(4,1)S(1)}, pred[2]{0:T(512)(128)(4,1)}, u32[]{:S(2)}) copy-start(pred[2]{0:T(512)(128)(4,1)} %get-tuple-element.46) | copy-start | bytes 10
  111.5 15.7 %copy-start.29 = (s32[2]{0:T(128)S(1)}, s32[2]{0:T(128)}, u32[]{:S(2)}) copy-start(s32[2]{0:T(128)} %get-tuple-element.7) | copy-start | bytes 28
  111.5 15.7 %copy-start.33 = (pred[2]{0:T(512)(128)(4,1)S(1)}, pred[2]{0:T(512)(128)(4,1)}, u32[]{:S(2)}) copy-start(pred[2]{0:T(512)(128)(4,1)} %get-tuple-element.45) | copy-start | bytes 10
  111.5 18.3 %copy-start.28 = (pred[2]{0:T(512)(128)(4,1)S(1)}, pred[2]{0:T(512)(128)(4,1)}, u32[]{:S(2)}) copy-start(pred[2]{0:T(512)(128)(4,1)} %get-tuple-element.49) | copy-start | bytes 10
  112.3 19.0 %copy-start.1 = (f32[2,2,7,16384]{3,1,0,2:T(2,128)}, f32[2,2,7,16384]{3,1,0,2:T(2,128)S(1)}, u32[]{:S(2)}) copy-start(f32[2,2,7,16384]{3,1,0,2:T(2,128)S(1)} %copy_dynamic-update-slice_fusion) | copy-start | bytes 5505028
  113.0 20.3 %copy-start.3 = (bf16[2,128,896]{1,2,0:T(8,128)(2,1)S(1)}, bf16[2,128,896]{1,2,0:T(8,128)(2,1)}, u32[]{:S(2)}) copy-start(bf16[2,128,896]{1,2,0:T(8,128)(2,1)} %copy-done.2) | copy-start | bytes 1376260
  113.0 22.6 %collective-permute-start.13 = (f32[2,2,16384]{2,1,0:T(2,128)S(1)}, f32[2,2,16384]{2,1,0:T(2,128)S(1)}, u32[]{:S(2)}, u32[]{:S(2)}) collective-permute-start(f32[2,2,16384]{2,1,0:T(2,128)S(1)} %convolution_bitcast_fusion.4), channel_id=1, source_target_pairs={{16,0},{24,8},{32,16},{40,24},{48,32},{56,40},{64,48},{72,56},{80,... | collective-permute-start | bytes 786440 | tf_op jit(solution)/shard_map/ppermute | solution.py:37
  117.4 18.3 %collective-permute-start.14 = (f32[2,2,16384]{2,1,0:T(2,128)S(1)}, f32[2,2,16384]{2,1,0:T(2,128)S(1)}, u32[]{:S(2)}, u32[]{:S(2)}) collective-permute-start(f32[2,2,16384]{2,1,0:T(2,128)S(1)} %convolution_bitcast_fusion.3), channel_id=1, source_target_pairs={{32,0},{40,8},{48,16},{56,24},{64,32},{72,40},{80,48},{88,56},{96,... | collective-permute-start | bytes 786440 | tf_op jit(solution)/shard_map/ppermute | solution.py:37
  123.9 9.7 %copy-start.24 = (bf16[2,128,1,128]{3,1,0,2:T(8,128)(2,1)S(1)}, bf16[2,128,1,128]{3,1,0,2:T(8,128)(2,1)}, u32[]{:S(2)}) copy-start(bf16[2,128,1,128]{3,1,0,2:T(8,128)(2,1)} %fusion.34) | copy-start | bytes 196612
  123.9 9.7 %copy-start.25 = (bf16[2,128,1,128]{3,1,0,2:T(8,128)(2,1)S(1)}, bf16[2,128,1,128]{3,1,0,2:T(8,128)(2,1)}, u32[]{:S(2)}) copy-start(bf16[2,128,1,128]{3,1,0,2:T(8,128)(2,1)} %fusion.35) | copy-start | bytes 196612
  123.9 9.7 %copy-start.26 = (bf16[2,128,1,128]{3,1,0,2:T(8,128)(2,1)S(1)}, bf16[2,128,1,128]{3,1,0,2:T(8,128)(2,1)}, u32[]{:S(2)}) copy-start(bf16[2,128,1,128]{3,1,0,2:T(8,128)(2,1)} %fusion.36) | copy-start | bytes 196612
  125.3 14.8 %collective-permute-start.15 = (f32[2,2,16384]{2,1,0:T(2,128)}, f32[2,2,16384]{2,1,0:T(2,128)S(1)}, u32[]{:S(2)}, u32[]{:S(2)}) collective-permute-start(f32[2,2,16384]{2,1,0:T(2,128)} %convolution_bitcast_fusion.2), channel_id=1, source_target_pairs={{64,0},{72,8},{80,16},{88,24},{96,32},{104,40},{112,48},{120,56},{... | collective-permute-start | bytes 786440 | tf_op jit(solution)/shard_map/ppermute | solution.py:37
  128.6 11.6 %collective-permute-start.16 = (f32[2,2,16384]{2,1,0:T(2,128)}, f32[2,2,16384]{2,1,0:T(2,128)S(1)}, u32[]{:S(2)}, u32[]{:S(2)}) collective-permute-start(f32[2,2,16384]{2,1,0:T(2,128)} %convolution_bitcast_fusion.1), channel_id=1, source_target_pairs={{128,0},{136,8},{144,16},{152,24},{160,32},{168,40},{176,48},{184,... | collective-permute-start | bytes 786440 | tf_op jit(solution)/shard_map/ppermute | solution.py:37
  131.3 14.4 %collective-permute-start.12 = (f32[2,2,16384]{2,1,0:T(2,128)S(1)}, f32[2,2,16384]{2,1,0:T(2,128)S(1)}, u32[]{:S(2)}, u32[]{:S(2)}) collective-permute-start(f32[2,2,16384]{2,1,0:T(2,128)S(1)} %fusion.4), channel_id=1, source_target_pairs={{8,0},{16,8},{24,16},{32,24},{40,32},{48,40},{56,48},{64,56},{72,6... | collective-permute-start | bytes 786440 | tf_op jit(solution)/shard_map/ppermute | solution.py:37
  (29 other events, 87.6 us)
